TPU v7x, 256 devices: a whole 4x4x8 slice. The times are simulated.
256 devices in a mesh: seq: 64 (over z, x, y_lo), head: 4 (over y_hi, core).
Axes of the slice: x: 4, y: 4 (y_hi: 2, y_lo: 2; y = y_hi * 2 + y_lo), z: 8, core: 2. Of those that a mesh axis runs over, the one named last changes fastest.
Arguments:
- query: bfloat16 [8192, 3072], P('seq', 'head'), may hold values from -256 to 256
- keys: bfloat16 [8192, 3072], P('seq', 'head'), may hold values from -4 to 4
- values: bfloat16 [8192, 3072], P('seq', 'head'), may hold values from -5 to 5
- out_weight: bfloat16 [3072, 4096], P('head'), may hold values from -0.109375 to 0.109375
- image_start: int32 [3], replicated, may hold values from 0 to 7168, as said below
Outputs:
- mixed: bfloat16 [8192, 4096], P('seq', 'head')
Inputs may be any that keep to these rules, and one draw needn't show every extreme that they name: `image_start`: the starts increase; each image's 1024 positions lie inside the sequence and no two images share a position; the last image ends at the sequence's end.
All inputs are finite; a program needn't handle non-finite values.
Results may differ from a plain program's by a relative error of at most 0.012.
Values may be sent and summed in bfloat16 or wider, within the bound.
A program may use at most 192 MiB of HBM per device.

v0:
```python
import jax
import jax.numpy as jnp
from jax import lax
from jax.sharding import PartitionSpec as P

HEAD_DIM = 128


def image_tags(positions, image_start, patch_count):
    inside = (positions[:, None] >= image_start[None, :]) & (
        positions[:, None] < image_start[None, :] + patch_count
    )
    labels = jnp.arange(image_start.shape[0], dtype=jnp.int32) + 1
    return jnp.sum(jnp.where(inside, labels[None, :], 0), axis=1) - 1


def body(query, keys, values, out_weight, image_start):
    cycle_size = lax.axis_size("seq")
    own_index = lax.axis_index("seq")
    row_count = query.shape[0]
    seq_total = row_count * cycle_size
    patch_count = min(1024, seq_total // 8)
    head_count = query.shape[1] // HEAD_DIM
    scale = HEAD_DIM ** (-0.5)
    query_pos = own_index * row_count + jnp.arange(row_count, dtype=jnp.int32)
    query_heads = jnp.transpose(query.reshape(row_count, head_count, HEAD_DIM), (1, 0, 2))
    query_tag = image_tags(query_pos, image_start, patch_count)
    initial = (
        jnp.full((head_count, row_count), -1e30, jnp.float32),
        jnp.zeros((head_count, row_count), jnp.float32),
        jnp.zeros((head_count, row_count, HEAD_DIM), jnp.float32),
    )
    key_major = jnp.transpose(keys.reshape(row_count, head_count, HEAD_DIM), (1, 0, 2))
    value_major = jnp.transpose(values.reshape(row_count, head_count, HEAD_DIM), (1, 0, 2))
    key_value = jnp.stack((key_major, value_major))
    block_pair = lax.all_gather(key_value, "seq", axis=2, tiled=True)
    piece_len = block_pair.shape[2]
    key_pos = jnp.arange(piece_len, dtype=jnp.int32)
    key_tag = image_tags(key_pos, image_start, patch_count)
    in_range = (key_pos >= 0) & (key_pos < seq_total)
    visible = in_range[None, :] & (
        (key_pos[None, :] <= query_pos[:, None])
        | (query_tag[:, None] == key_tag[None, :]) & (query_tag[:, None] >= 0)
    )

    def compute(state_old):
        row_high, row_sum, weighted = state_old
        key_block = block_pair[0]
        value_block = block_pair[1]
        scores = (
            jnp.einsum("hqd,hkd->hqk", query_heads, key_block, preferred_element_type=jnp.float32)
            * scale
        )
        scores = jnp.where(visible[None], scores, -1e30)
        new_high = jnp.maximum(row_high, jnp.max(scores, axis=-1))
        weights = jnp.where(visible[None], jnp.exp(scores - new_high[..., None]), 0.0)
        row_sum = jnp.sum(weights, axis=-1)
        update = jnp.einsum(
            "hqk,hkd->hqd",
            weights.astype(jnp.bfloat16),
            value_block,
            preferred_element_type=jnp.float32,
        )
        weighted = update
        return (new_high, row_sum, weighted)

    def unchanged(state_old):
        return state_old

    state_now = lax.cond(jnp.any(visible), compute, unchanged, initial)
    row_high, row_sum, weighted = state_now
    attended = (weighted / row_sum[..., None]).astype(jnp.bfloat16)
    attended_rows = jnp.transpose(attended, (1, 0, 2)).reshape(row_count, head_count * HEAD_DIM)
    partial_value = jnp.dot(attended_rows, out_weight, preferred_element_type=jnp.float32)
    return lax.psum_scatter(
        partial_value.astype(jnp.bfloat16), "head", scatter_dimension=1, tiled=True
    )


def solution(mesh):
    placed = (P("seq", "head"), P("seq", "head"), P("seq", "head"), P("head", None), P())
    return jax.shard_map(
        body, mesh=mesh, in_specs=placed, out_specs=P("seq", "head"), check_vma=False
    )
```

profile of v0, /device:TPU:1, one launch (start us, length us, event | category | flops | bytes accessed | tf_op | source)
XLA Modules:
  0.0 784.2 jit_solution(2414290603275093940)
XLA Ops:
  6.5 0.0 all-gather.2.cloned.1.call-start
  6.5 1.1 copy.12
  7.6 1.1 copy.13
  8.7 0.8 pad_maximum_fusion
  9.6 0.0 all-gather.2.cloned.1.call-update
  9.6 0.0 reduce-scatter.2.cloned.1.call-start
  9.6 1.1 copy.14
  10.8 0.7 iota_add_fusion
  11.4 0.7 select_reduce_fusion.1
  12.2 0.8 select_reduce_fusion
  13.0 2.6 fusion.16
  16.3 603.2 %all-gather.2.cloned.1.call-done = bf16[2,6,8192,128]{2,3,1,0:T(8,128)(2,1)} async-done(((bf16[2,6,128,128]{2,3,1,0:T(8,128)(2,1)}), bf16[2,6,8192,128]{2,3,1,0:T(8,128)(2,1)}) %all-gather.2.cloned.1.call-update) | async-done | bytes 25165840 | tf_op jit(solution)/shard_map/all_gather | solution.py:36
  619.5 74.4 %conditional.1 = (f32[6,128]{1,0:T(8,128)S(1)}, f32[6,128,128]{1,2,0:T(8,128)S(1)}) conditional(s32[]{:T(128)} %convert_element_type.12, () %tuple.13, (pred[128,8192]{1,0:T(8,128)(4,1)S(1)}, bf16[2,6,8192,128]{2,3,1,0:T(8,128)(2,1)}, bf16[6,128,128]{1,2,0:T(8,128)(2,1)S(1)}) %tuple.28), branch_computations={%region_3.4_spmd, %region_4.7_spmd} | conditional | flops 3303013632 | bytes 154748944 | solution.py:70
  619.5 32.6 %copy.15 = bf16[2,6,8192,128]{3,2,1,0:T(8,128)(2,1)} copy(bf16[2,6,8192,128]{2,3,1,0:T(8,128)(2,1)} %get-tuple-element.22) | data formatting | bytes 50331648 | tf_op jit(solution)/shard_map
  652.1 13.6 %fusion = (f32[6,128]{1,0:T(8,128)S(1)}, f32[6,128,8192]{2,1,0:T(8,128)}) fusion(pred[128,8192]{1,0:T(8,128)(4,1)S(1)} %get-tuple-element.11, bf16[6,128,128]{1,2,0:T(8,128)(2,1)S(1)} %get-tuple-element.23, bf16[2,6,8192,128]{3,2,1,0:T(8,128)(2,1)} %copy.15), kind=kOutput, calls=%fused_computation.2 | convolution fusion | flops 1629486336 | bytes 38996992 | tf_op jit(solution)/shard_map/cond/branch_1_fun/hqd,hkd->hqk/dot_general | solution.py:51
  665.7 15.8 %fusion.3 = f32[6,128,128]{1,2,0:T(8,128)S(1)} fusion(bf16[2,6,8192,128]{3,2,1,0:T(8,128)(2,1)} %copy.15, f32[6,128,8192]{2,1,0:T(8,128)} %get-tuple-element.28, f32[6,128]{1,0:T(8,128)S(1)} %broadcast_maximum_fusion, pred[128,8192]{1,0:T(8,128)(4,1)S(1)} %get-tuple-element.11), kind=kOutput, calls=%fused_computation.6 | convolution fusion | flops 1642070016 | bytes 39193600 | tf_op jit(solution)/shard_map/cond | solution.py:70
  681.4 12.5 %fusion.2 = f32[6,128]{1,0:T(8,128)S(1)} fusion(f32[6,128,8192]{2,1,0:T(8,128)} %get-tuple-element.28, f32[6,128]{1,0:T(8,128)S(1)} %broadcast_maximum_fusion, pred[128,8192]{1,0:T(8,128)(4,1)S(1)} %get-tuple-element.11), kind=kLoop, calls=%fused_computation.4 | loop fusion | flops 31456512 | bytes 26220544 | tf_op jit(solution)/shard_map/cond/branch_1_fun/reduce_sum | solution.py:57
  693.9 4.8 convolution_convert_fusion
  698.7 0.0 reduce-scatter.2.cloned.1.call-update
  698.8 78.6 %reduce-scatter.2.cloned.1.call-done = bf16[128,1024]{1,0:T(8,128)(2,1)} async-done(((bf16[128,4096]{1,0:T(8,128)(2,1)}), bf16[128,1024]{1,0:T(8,128)(2,1)}) %reduce-scatter.2.cloned.1.call-update) | async-done | bytes 262160 | tf_op jit(solution)/shard_map/reduce_scatter | solution.py:75
  (7 shorter events, 0.1 us)
Async XLA Ops:
  6.5 612.9 %all-gather.2.cloned.1.call-start = ((), (), s32[]{:S(2)}) async-start(), calls=%async_computation.1 | async-start | bytes 25559040 | tf_op jit(solution)/shard_map/all_gather | solution.py:36
  9.6 767.8 %reduce-scatter.2.cloned.1.call-start = ((), (), s32[]{:S(2)}) async-start(), calls=%async_computation.2 | async-start | bytes 1310720 | tf_op jit(solution)/shard_map/reduce_scatter | solution.py:75
Sparse Core Ops, SparseCore 0:
  9.7 609.7 all-gather.1
  698.9 78.4 reduce-scatter.1
where the time goes:
time: 785 us; the launch traced here: 784 us
  waiting for transfers between devices  682 us (87%)
  local copies, waits for them, and re-layouts  35.8 us (5%)
  matrix products  34.2 us (4%)
  other arithmetic  18.2 us (2%)
  between operations  14.1 us (2%)
    all_gather x1, waiting for transfers between devices, body(): block_pair = lax.all_gather(key_value, 'seq', axis=2, tiled=True)  603 us
    reduce_scatter x1, waiting for transfers between devices, body(): lax.psum_scatter(partial_value.astype(jnp.bfloat16), 'head', scatter_dime...  78.6 us
    another operation x1, local copies, waits for them, and re-layouts  32.6 us
    cond x1, matrix products, body(): state_now = lax.cond(jnp.any(visible), compute, unchanged, initial)  15.8 us
  transfers between devices with their start and end apart: 2, of which 2 were waited for; matrix products, arithmetic and copies ran while one was open for 1% of the time, Pallas kernels for 0%

commit v1 on v0

--- a/solution.py
+++ b/solution.py
@@ -33,7 +33,9 @@
     key_major = jnp.transpose(keys.reshape(row_count, head_count, HEAD_DIM), (1, 0, 2))
     value_major = jnp.transpose(values.reshape(row_count, head_count, HEAD_DIM), (1, 0, 2))
     key_value = jnp.stack((key_major, value_major))
-    block_pair = lax.all_gather(key_value, "seq", axis=2, tiled=True)
+    block_pair = jnp.concatenate(
+        lax.all_to_all(jnp.stack([key_value] * lax.axis_size("seq")), "seq", 0, 0), axis=2
+    )
     piece_len = block_pair.shape[2]
     key_pos = jnp.arange(piece_len, dtype=jnp.int32)
     key_tag = image_tags(key_pos, image_start, patch_count)

time: 785 us -> 756 us (0.963)
  waiting for transfers between devices: 682 us -> 649 us
  starting transfers between devices: 0.04 us -> 13.9 us
    all_gather x1 -> x0, waiting for transfers between devices: 603 us -> none  [body(): block_pair = lax.all_gather(key_value, 'seq', axis=2, tiled=True)]
    all_to_all x0 -> x1, waiting for transfers between devices: none -> 582 us  [body(): lax.all_to_all(jnp.stack([key_value] * lax.axis_size('seq')), 'seq', 0, 0)]
    another operation x1 -> x2, local copies, waits for them, and re-layouts: 32.6 us -> 9.28 us  [the longest x1 9.05 us: body(): jnp.stack([key_value] * lax.axis_size('seq'))]
    slice x0 -> x1, local copies, waits for them, and re-layouts: none -> 17.8 us  [compute(): value_block = block_pair[1]]
    all_to_all x0 -> x1, starting transfers between devices: none -> 13.8 us  [body(): lax.all_to_all(jnp.stack([key_value] * lax.axis_size('seq')), 'seq', 0, 0)]
    reduce_scatter x1, waiting for transfers between devices: 78.6 us -> 67 us  [body(): lax.psum_scatter(partial_value.astype(jnp.bfloat16), 'head', scatter_dime...]
  transfers between devices with their start and end apart: 2 -> 2, of which waited for: 2 -> 2; matrix products, arithmetic and copies ran while one was open for 1% -> 0% of each run, Pallas kernels for 0% -> 0%
where the time goes in v1:
time: 756 us
  waiting for transfers between devices  649 us (86%)
  matrix products  34.1 us (5%)
  local copies, waits for them, and re-layouts  29.4 us (4%)
  other arithmetic  15.4 us (2%)
  between operations  14.2 us (2%)
  starting transfers between devices  13.9 us (2%)
    all_to_all x1, waiting for transfers between devices, body(): lax.all_to_all(jnp.stack([key_value] * lax.axis_size('seq')), 'seq', 0, 0)  582 us
    reduce_scatter x1, waiting for transfers between devices, body(): lax.psum_scatter(partial_value.astype(jnp.bfloat16), 'head', scatter_dime...  67 us
    slice x1, local copies, waits for them, and re-layouts, compute(): value_block = block_pair[1]  17.8 us
    cond x1, matrix products, body(): state_now = lax.cond(jnp.any(visible), compute, unchanged, initial)  15.8 us
  transfers between devices with their start and end apart: 2, of which 2 were waited for; matrix products, arithmetic and copies ran while one was open for 0% of the time, Pallas kernels for 0%

profile of v1, /device:TPU:1, one launch (start us, length us, event | category | flops | bytes accessed | tf_op | source)
XLA Modules:
  0.0 755.8 jit_solution(1255880501721343532)
XLA Ops:
  6.5 1.1 copy.21
  7.6 1.1 copy.22
  8.8 0.2 copy.23
  9.0 9.1 %stack.11 = bf16[64,2,6,128,128]{4,3,2,1,0:T(8,128)(2,1)} broadcast(bf16[2,6,128,128]{3,2,1,0:T(8,128)(2,1)S(1)} %copy.23), dimensions={1,2,3,4} | broadcast | bytes 25559040 | tf_op jit(solution)/shard_map/stack | solution.py:37
  18.1 0.0 copy-start
  18.1 0.0 copy-start.1
  18.1 13.8 %all-to-all-start = ((bf16[64,2,6,128,128]{4,3,2,1,0:T(8,128)(2,1)}), bf16[64,2,6,128,128]{4,3,2,1,0:T(8,128)(2,1)}, u32[]{:S(2)}, u32[]{:S(2)}) async-start(bf16[64,2,6,128,128]{4,3,2,1,0:T(8,128)(2,1)} %stack.11), calls=%async_computation | async-start | bytes 50331648 | tf_op jit(solution)/shard_map/all_to_all | solution.py:37
  31.9 0.0 reduce-scatter.2.cloned.1.call-start
  32.0 0.0 copy-done
  32.0 0.2 copy.24
  32.2 0.0 copy-done.1
  32.2 0.1 select_reduce_fusion.1
  32.3 0.2 select_reduce_fusion
  32.5 2.6 fusion.12
  35.7 581.8 %all-to-all-done = bf16[64,2,6,128,128]{4,3,2,1,0:T(8,128)(2,1)} async-done(((bf16[64,2,6,128,128]{4,3,2,1,0:T(8,128)(2,1)}), bf16[64,2,6,128,128]{4,3,2,1,0:T(8,128)(2,1)}, u32[]{:S(2)}, u32[]{:S(2)}) %all-to-all-start) | async-done | bytes 25165856 | tf_op jit(solution)/shard_map/all_to_all | solution.py:37
  617.5 59.6 %conditional.1 = (f32[6,128]{1,0:T(8,128)S(1)}, f32[6,128,128]{1,2,0:T(8,128)S(1)}) conditional(s32[]{:T(128)} %convert_element_type.12, () %tuple.13, (pred[128,8192]{1,0:T(8,128)(4,1)S(1)}, bf16[2,6,64,128,128]{4,3,1,0,2:T(8,128)(2,1)}, bf16[6,128,128]{1,2,0:T(8,128)(2,1)S(1)}) %tuple.28), branch_computations={%region_3.4_spmd, %region_4.7_spmd} | conditional | flops 3303013632 | bytes 154748944 | solution.py:72
  617.5 17.8 %fusion.14 = (bf16[1,6,64,128,128]{4,3,2,1,0:T(8,128)(2,1)}, bf16[1,6,64,128,128]{4,3,2,1,0:T(8,128)(2,1)}) fusion(bf16[2,6,64,128,128]{4,3,1,0,2:T(8,128)(2,1)} %get-tuple-element.26), kind=kLoop, calls=%fused_computation.30 | loop fusion | bytes 50331648 | tf_op jit(solution)/shard_map/cond/branch_1_fun/slice | solution.py:51
  635.3 13.6 %fusion = (f32[6,128]{1,0:T(8,128)S(1)}, f32[6,128,8192]{2,1,0:T(8,128)}) fusion(pred[128,8192]{1,0:T(8,128)(4,1)S(1)} %get-tuple-element.12, bf16[6,128,128]{1,2,0:T(8,128)(2,1)S(1)} %get-tuple-element.27, bf16[6,8192,128]{2,1,0:T(8,128)(2,1)} %bitcast.24), kind=kOutput, calls=%fused_computation.2 | convolution fusion | flops 1629486336 | bytes 38996992 | tf_op jit(solution)/shard_map/cond/branch_1_fun/hqd,hkd->hqk/dot_general | solution.py:53
  648.9 15.8 %fusion.3 = f32[6,128,128]{1,2,0:T(8,128)S(1)} fusion(bf16[6,8192,128]{2,1,0:T(8,128)(2,1)} %bitcast.25, f32[6,128,8192]{2,1,0:T(8,128)} %get-tuple-element.34, f32[6,128]{1,0:T(8,128)S(1)} %broadcast_maximum_fusion, pred[128,8192]{1,0:T(8,128)(4,1)S(1)} %get-tuple-element.12), kind=kOutput, calls=%fused_computation.5 | convolution fusion | flops 1642070016 | bytes 39193600 | tf_op jit(solution)/shard_map/cond | solution.py:72
  664.7 12.5 %fusion.2 = f32[6,128]{1,0:T(8,128)S(1)} fusion(f32[6,128,8192]{2,1,0:T(8,128)} %get-tuple-element.34, f32[6,128]{1,0:T(8,128)S(1)} %broadcast_maximum_fusion, pred[128,8192]{1,0:T(8,128)(4,1)S(1)} %get-tuple-element.12), kind=kLoop, calls=%fused_computation.4 | loop fusion | flops 31456512 | bytes 26220544 | tf_op jit(solution)/shard_map/cond/branch_1_fun/reduce_sum | solution.py:59
  677.2 4.8 convolution_convert_fusion
  682.0 0.0 reduce-scatter.2.cloned.1.call-update
  682.0 67.0 %reduce-scatter.2.cloned.1.call-done = bf16[128,1024]{1,0:T(8,128)(2,1)} async-done(((bf16[128,4096]{1,0:T(8,128)(2,1)}), bf16[128,1024]{1,0:T(8,128)(2,1)}) %reduce-scatter.2.cloned.1.call-update) | async-done | bytes 262160 | tf_op jit(solution)/shard_map/reduce_scatter | solution.py:77
  (9 shorter events, 0.1 us)
Async XLA Ops:
  18.1 13.9 %copy-start = (bf16[128,768]{1,0:T(8,128)(2,1)S(1)}, bf16[128,768]{1,0:T(8,128)(2,1)}, u32[]{:S(2)}) copy-start(bf16[128,768]{1,0:T(8,128)(2,1)} %param.7) | copy-start | bytes 589828
  18.1 14.1 %copy-start.1 = (s32[3]{0:T(128)S(1)}, s32[3]{0:T(128)}, u32[]{:S(2)}) copy-start(s32[3]{0:T(128)} %param.11) | copy-start | bytes 40
  18.1 599.5 %all-to-all-start = ((bf16[64,2,6,128,128]{4,3,2,1,0:T(8,128)(2,1)}), bf16[64,2,6,128,128]{4,3,2,1,0:T(8,128)(2,1)}, u32[]{:S(2)}, u32[]{:S(2)}) async-start(bf16[64,2,6,128,128]{4,3,2,1,0:T(8,128)(2,1)} %stack.11), calls=%async_computation | async-start | bytes 50331648 | tf_op jit(solution)/shard_map/all_to_all | solution.py:37
  31.9 717.1 %reduce-scatter.2.cloned.1.call-start = ((), (), s32[]{:S(2)}) async-start(), calls=%async_computation.2 | async-start | bytes 1310720 | tf_op jit(solution)/shard_map/reduce_scatter | solution.py:77
Sparse Core Ops, SparseCore 0:
  682.1 66.8 reduce-scatter.1
